TPU v7x, 128 devices: a whole 4x4x4 slice. The times are simulated.
128 devices in a mesh: grp: 8 (over x, core), seq: 16 (over y, z).
Axes of the slice: x: 4, y: 4, z: 4, core: 2. Of those that a mesh axis runs over, the one named last changes fastest.
Arguments:
- tokens: bfloat16 [32, 4, 5120], P(None, None, ('grp', 'seq')), may hold values from -90 to 90
- lengths: int32 [32], replicated, may hold values from 1 to 16384, as said below
- group_perm: int32 [32], replicated, may hold values from 0 to 31, as said below
- page_table: int32 [32, 128], replicated, may hold values from 0 to 31, as said below
- k_pool: bfloat16 [4096, 128, 1024], P(('grp', 'seq')), may hold values from -17 to 17
- v_pool: bfloat16 [4096, 128, 1024], P(('grp', 'seq')), may hold values from -7 to 7
- gain_in: float32 [5120], P(('grp', 'seq')), may hold values from 0.25 to 1.75
- qkv_weight: bfloat16 [5120, 7168], P('grp', 'seq'), may hold values from -0.15625 to 0.15625
- qkv_bias: float32 [7168], P('seq'), may hold values from -16 to 16
- o_weight: bfloat16 [5120, 5120], P('seq', 'grp'), may hold values from -0.078125 to 0.078125
- gain_mid: float32 [5120], P(('grp', 'seq')), may hold values from 0.25 to 1.75
- gate_weight: bfloat16 [5120, 13824], P('grp', 'seq'), may hold values from -0.078125 to 0.078125
- up_weight: bfloat16 [5120, 13824], P('grp', 'seq'), may hold values from -0.078125 to 0.078125
- down_weight: bfloat16 [13824, 5120], P('seq', 'grp'), may hold values from -0.0546875 to 0.0546875
Outputs:
- mixed: bfloat16 [32, 4, 5120], P(None, None, ('grp', 'seq'))
Inputs may be any that keep to these rules, and one draw needn't show every extreme that they name: `lengths`: one request holds exactly 16384 cached tokens. A permutation of the requests; request group_perm[i] belongs to group i // 4. `page_table`: page p of request r lies on the device with grp index g and seq index p // 8, where g is the group of r; the slots named for one device are all different.
All inputs are finite; a program needn't handle non-finite values.
Results may differ from a plain program's by a relative error of at most 0.015.
Values may be sent and summed in bfloat16 or wider, within the bound.
No kernel may reach another device: no remote copies, remote signals or barrier semaphores. Data moves between devices by JAX's collectives and lax.ppermute only.
A program may use at most 128 MiB of HBM per device.

v0:
```python
import jax
import jax.numpy as jnp
from jax import lax
from jax.sharding import PartitionSpec as P

D = 5120
HEADS = 40
KV_HEADS = 8
HEAD_DIM = 128
STEPS = 4
REQ_GRP = 4
SHARD_PAGES = 8
PAGE = 128
BLOCK_PAGES = 4
EPSILON = 1e-06
LOW_SCORE = -1e30
ROPE_BASE = 1000000.0


def rotary(values, position):
    half_dim = values.shape[-1] // 2
    exponent = jnp.arange(half_dim, dtype=jnp.float32) * (2.0 / values.shape[-1])
    inverse = jnp.exp(-exponent * jnp.log(jnp.float32(ROPE_BASE)))
    angle = position[..., None, None] * inverse
    cosine = jnp.cos(angle)
    sine_part = jnp.sin(angle)
    first_half = values[..., :half_dim]
    second_half = values[..., half_dim:]
    return jnp.concatenate(
        [
            first_half * cosine - second_half * sine_part,
            second_half * cosine + first_half * sine_part,
        ],
        axis=-1,
    )


def absorb(carried, query_mat, key_block, value_block, live_mask, score_scale):
    best_score, weight_sums, weighted = carried
    scores = (
        jnp.einsum("hqd,khd->hqk", query_mat, key_block, preferred_element_type=jnp.float32)
        * score_scale
    )
    scores = jnp.where(live_mask, scores, LOW_SCORE)
    fresh_top = jnp.maximum(best_score, jnp.max(scores, axis=-1))
    rescale = jnp.exp(best_score - fresh_top)
    weights = jnp.where(live_mask, jnp.exp(scores - fresh_top[..., None]), 0.0)
    weight_sums = weight_sums * rescale + jnp.sum(weights, axis=-1)
    weighted = weighted * rescale[..., None] + jnp.einsum(
        "hqk,khd->hqd",
        weights.astype(jnp.bfloat16),
        value_block,
        preferred_element_type=jnp.float32,
    )
    return (fresh_top, weight_sums, weighted)


def body(
    tokens,
    lengths,
    group_perm,
    page_table,
    k_pool,
    v_pool,
    gain_in,
    qkv_weight,
    qkv_bias,
    o_weight,
    gain_mid,
    gate_weight,
    up_weight,
    down_weight,
):
    n_seq = lax.axis_size("seq")
    grp_idx = lax.axis_index("grp")
    seq_idx = lax.axis_index("seq")
    group_q = HEADS // KV_HEADS
    query_rows = STEPS * group_q
    q_width = HEADS * HEAD_DIM
    kv_width = KV_HEADS * HEAD_DIM
    score_scale = HEAD_DIM ** (-0.5)
    sorted_rows = jnp.take(tokens, group_perm, axis=0).astype(jnp.float32)
    squares_in = lax.psum(jnp.sum(sorted_rows * sorted_rows, axis=-1), ("grp", "seq"))
    normed_in = (sorted_rows * lax.rsqrt(squares_in / D + EPSILON)[..., None] * gain_in).astype(
        jnp.bfloat16
    )
    proj_part = jnp.einsum(
        "rtc,ck->rtk",
        lax.all_gather(normed_in, "seq", axis=2, tiled=True),
        qkv_weight,
        preferred_element_type=jnp.float32,
    )
    proj_share = (
        lax.psum_scatter(
            proj_part.astype(jnp.bfloat16), "grp", scatter_dimension=0, tiled=True
        ).astype(jnp.float32)
        + qkv_bias
    )
    proj_full = lax.all_gather(proj_share, "seq", axis=2, tiled=True)
    members = lax.dynamic_slice_in_dim(group_perm, grp_idx * REQ_GRP, REQ_GRP)
    my_lengths = jnp.take(lengths, members)
    steps_range = jnp.arange(STEPS, dtype=jnp.int32)
    position = (my_lengths[:, None] + steps_range[None, :]).astype(jnp.float32)
    queries = rotary(
        proj_full[..., :q_width].reshape(REQ_GRP, STEPS, HEADS, HEAD_DIM), position
    ).astype(jnp.bfloat16)
    new_keys = rotary(
        proj_full[..., q_width : q_width + kv_width].reshape(REQ_GRP, STEPS, KV_HEADS, HEAD_DIM),
        position,
    ).astype(jnp.bfloat16)
    new_values = (
        proj_full[..., q_width + kv_width :]
        .reshape(REQ_GRP, STEPS, KV_HEADS, HEAD_DIM)
        .astype(jnp.bfloat16)
    )
    shard_rows = SHARD_PAGES * PAGE
    block_rows = BLOCK_PAGES * PAGE
    shard_base = seq_idx * shard_rows
    slot_table = lax.dynamic_slice_in_dim(
        jnp.take(page_table, members, axis=0), seq_idx * SHARD_PAGES, SHARD_PAGES, 1
    )
    is_last = seq_idx == n_seq - 1
    causal = (
        steps_range[None, :] <= (jnp.arange(query_rows, dtype=jnp.int32) // group_q)[:, None]
    ) & is_last
    causal = causal[None]
    query_all = (
        queries.reshape(REQ_GRP, STEPS, KV_HEADS, group_q, HEAD_DIM)
        .transpose(0, 2, 1, 3, 4)
        .reshape(REQ_GRP, KV_HEADS, query_rows, HEAD_DIM)
    )
    live_all = jnp.clip(my_lengths - shard_base, 0, shard_rows)
    block_offsets = jnp.arange(block_rows, dtype=jnp.int32)
    best_list = []
    sums_list = []
    acc_list = []
    for member in range(REQ_GRP):
        query_mat = query_all[member]
        length = my_lengths[member]
        member_slots = slot_table[member]
        initial = (
            jnp.full((KV_HEADS, query_rows), LOW_SCORE, jnp.float32),
            jnp.zeros((KV_HEADS, query_rows), jnp.float32),
            jnp.zeros((KV_HEADS, query_rows, HEAD_DIM), jnp.float32),
        )
        carried = absorb(
            initial, query_mat, new_keys[member], new_values[member], causal, score_scale
        )
        block_count = (live_all[member] + block_rows - 1) // block_rows

        def advance(
            block_index, running, member_slots=member_slots, length=length, query_mat=query_mat
        ):
            slot_ids = lax.dynamic_slice_in_dim(
                member_slots, block_index * BLOCK_PAGES, BLOCK_PAGES
            )
            key_block = jnp.take(k_pool, slot_ids, axis=0).reshape(block_rows, KV_HEADS, HEAD_DIM)
            value_block = jnp.take(v_pool, slot_ids, axis=0).reshape(block_rows, KV_HEADS, HEAD_DIM)
            positions = shard_base + block_index * block_rows + block_offsets
            return absorb(
                running,
                query_mat,
                key_block,
                value_block,
                (positions < length)[None, None, :],
                score_scale,
            )

        carried = lax.fori_loop(0, block_count, advance, carried)
        best_list.append(carried[0])
        sums_list.append(carried[1])
        acc_list.append(carried[2])
    best_score = jnp.stack(best_list)
    weight_sums = jnp.stack(sums_list)
    weighted = jnp.stack(acc_list)
    top_score = lax.pmax(best_score, "seq")
    factor = jnp.exp(best_score - top_score)
    weight_sums, weighted = (
        lax.psum((weight_sums * factor).astype(jnp.bfloat16), "seq").astype(jnp.float32),
        lax.psum((weighted * factor[..., None]).astype(jnp.bfloat16), "seq").astype(jnp.float32),
    )
    attended = (weighted / weight_sums[..., None]).reshape(
        REQ_GRP, KV_HEADS, STEPS, group_q, HEAD_DIM
    )
    attended = (
        attended.transpose(0, 2, 1, 3, 4).reshape(REQ_GRP, STEPS, q_width).astype(jnp.bfloat16)
    )
    out_width = o_weight.shape[0]
    attended_cols = lax.dynamic_slice_in_dim(attended, seq_idx * out_width, out_width, 2)
    out_terms = jnp.einsum(
        "rtc,cd->rtd",
        lax.all_gather(attended_cols, "grp", axis=0, tiled=True),
        o_weight,
        preferred_element_type=jnp.float32,
    )
    attn_sum = lax.psum_scatter(
        out_terms.astype(jnp.bfloat16), "seq", scatter_dimension=2, tiled=True
    ).astype(jnp.float32)
    residual = sorted_rows + attn_sum
    squares_mid = lax.psum(jnp.sum(residual * residual, axis=-1), ("grp", "seq"))
    normed_mid = (residual * lax.rsqrt(squares_mid / D + EPSILON)[..., None] * gain_mid).astype(
        jnp.bfloat16
    )
    segment = lax.all_gather(normed_mid, "seq", axis=2, tiled=True)
    gate_part = jnp.einsum("rtc,cf->rtf", segment, gate_weight, preferred_element_type=jnp.float32)
    up_part = jnp.einsum("rtc,cf->rtf", segment, up_weight, preferred_element_type=jnp.float32)
    gate_sum, up_sum = (
        lax.psum(gate_part.astype(jnp.bfloat16), "grp").astype(jnp.float32),
        lax.psum(up_part.astype(jnp.bfloat16), "grp").astype(jnp.float32),
    )
    hidden = (jax.nn.silu(gate_sum) * up_sum).astype(jnp.bfloat16)
    down_terms = jnp.einsum("rtf,fd->rtd", hidden, down_weight, preferred_element_type=jnp.float32)
    down_sum = lax.psum_scatter(
        down_terms.astype(jnp.bfloat16), "seq", scatter_dimension=2, tiled=True
    ).astype(jnp.float32)
    restore = jnp.argsort(group_perm)
    return jnp.take(residual + down_sum, restore, axis=0).astype(jnp.bfloat16)


def solution(mesh):
    return jax.shard_map(
        body,
        mesh=mesh,
        in_specs=(
            P(None, None, ("grp", "seq")),
            P(),
            P(),
            P(),
            P(("grp", "seq"), None, None),
            P(("grp", "seq"), None, None),
            P(("grp", "seq")),
            P("grp", "seq"),
            P("seq"),
            P("seq", "grp"),
            P(("grp", "seq")),
            P("grp", "seq"),
            P("grp", "seq"),
            P("seq", "grp"),
        ),
        out_specs=P(None, None, ("grp", "seq")),
        check_vma=False,
    )
```

profile of v0, /device:TPU:0, one launch (start us, length us, event | category | flops | bytes accessed | tf_op | source)
XLA Modules:
  0.0 875.4 jit_solution(11767665669221930165)
XLA Ops:
  6.5 0.8 compare_and_fusion.5
  8.0 1.4 gather_fusion.8
  9.5 68.2 %psum.42 = f32[32,4]{0,1:T(4,128)S(1)} all-reduce(f32[32,4]{0,1:T(4,128)S(1)} %fusion.75), channel_id=1, replica_groups=mesh['grp'=8,'seq'=16] {'grp','seq'}, use_global_device_ids=true, to_apply=%region_2.3 | all-reduce | flops 128 | bytes 1024 | tf_op jit(solution)/shard_map/psum | solution.py:83
  78.6 21.7 %all_gather.12 = bf16[32,4,640]{0,1,2:T(4,128)(2,1)S(1)} all-gather(bf16[32,4,40]{0,1,2:T(4,128)(2,1)S(1)} %copy.177), channel_id=1, replica_groups=mesh['grp'=8,'seq'=16] {'seq'}, dimensions={2}, use_global_device_ids=true | all-gather | bytes 174080 | tf_op jit(solution)/shard_map/all_gather | solution.py:89
  100.3 2.2 convolution_convert_fusion.4
  103.4 1.3 gather_fusion.9
  104.7 1.3 gather_fusion.10
  110.1 1.2 dynamic-slice
  112.0 48.4 %all-reduce.12.cloned.1.call-done = bf16[32,4,448]{2,0,1:T(8,128)(2,1)} async-done(((bf16[32,4,448]{2,0,1:T(8,128)(2,1)}), bf16[32,4,448]{2,0,1:T(8,128)(2,1)}) %all-reduce.12.cloned.1.call-update) | async-done | bytes 114704
  160.5 0.8 convert_add_fusion.2
  161.7 80.0 %all_gather.13 = f32[4,4,7168]{1,0,2:T(4,128)S(1)} all-gather(f32[4,4,448]{1,0,2:T(4,128)S(1)} %copy.179), channel_id=1, replica_groups=mesh['grp'=8,'seq'=16] {'seq'}, dimensions={2}, use_global_device_ids=true | all-gather | bytes 487424 | tf_op jit(solution)/shard_map/all_gather | solution.py:99
  241.8 4.1 convert.21
  245.8 4.5 slice.158
  251.3 9.4 %fusion.141 = (f32[4,4,40,64]{1,0,3,2:T(4,128)}, f32[4,4,40,64]{1,0,3,2:T(4,128)}) fusion(f32[4,4,40,128]{1,0,3,2:T(4,128)} %bitcast.196), kind=kLoop, calls=%fused_computation.266 | loop fusion | bytes 655360 | tf_op jit(solution)/shard_map/slice | solution.py:28
  260.7 4.1 copy.227
  264.8 4.1 copy.226
  271.7 4.4 fusion.142
  276.2 0.9 copy.187
  277.4 0.9 copy.199
  280.1 22.0 %while.63 = (s32[]{:T(128)}, f32[8,20]{1,0:T(8,128)S(1)}, f32[8,20]{1,0:T(8,128)S(1)}, f32[8,20,128]{2,1,0:T(8,128)S(1)}, s32[]{:T(128)}, /*index=5*/s32[]{:T(12...) while((s32[]{:T(128)}, f32[8,20]{1,0:T(8,128)S(1)}, ...), condition=%wide.region_27.29_spmd.clone, body=%wide.region_24.28_spmd.clone.sunk | while | flops 43772256 | bytes 15884615 | solution.py:169
  280.9 4.0 gather_fusion.7
  284.9 4.0 gather_fusion.6
  289.5 0.7 fusion.203
  291.9 4.0 gather_fusion.7
  295.9 4.0 gather_fusion.6
  300.5 0.7 fusion.203
  302.2 1.3 exponential_multiply_fusion.2
  303.7 11.1 %while.61 = (s32[]{:T(128)}, f32[8,20]{1,0:T(8,128)S(1)}, f32[8,20]{1,0:T(8,128)S(1)}, f32[8,20,128]{2,1,0:T(8,128)S(1)}, s32[]{:T(128)}, /*index=5*/s32[]{:T(12...) while((s32[]{:T(128)}, f32[8,20]{1,0:T(8,128)S(1)}, ...), condition=%wide.region_15.17_spmd.clone, body=%wide.region_12.16_spmd.clone.sunk | while | flops 43772256 | bytes 15884615 | solution.py:169
  304.6 4.0 gather_fusion.3
  308.6 4.0 gather_fusion.2
  314.9 1.0 convolution_add_fusion.5
  315.8 12.8 %while.62 = (s32[]{:T(128)}, f32[8,20]{1,0:T(8,128)S(1)}, f32[8,20]{1,0:T(8,128)S(1)}, f32[8,20,128]{2,1,0:T(8,128)S(1)}, s32[]{:T(128)}, /*index=5*/s32[]{:T(12...) while((s32[]{:T(128)}, f32[8,20]{1,0:T(8,128)S(1)}, ...), condition=%wide.region_21.23_spmd.clone, body=%wide.region_18.22_spmd.clone.sunk | while | flops 43772256 | bytes 16048483 | solution.py:169
  316.6 1.2 compare_and_fusion.13
  317.8 4.0 gather_fusion.5
  321.8 4.0 gather_fusion.4
  325.8 0.9 broadcast_select_fusion.17
  329.3 0.9 convolution_add_fusion.7
  330.3 23.8 %while.60 = (s32[]{:T(128)}, f32[8,20]{1,0:T(8,128)S(1)}, f32[8,20]{1,0:T(8,128)S(1)}, f32[8,20,128]{2,1,0:T(8,128)S(1)}, s32[]{:T(128)}, /*index=5*/s32[]{:T(12...) while((s32[]{:T(128)}, f32[8,20]{1,0:T(8,128)S(1)}, ...), condition=%wide.region_9.11_spmd.clone, body=%wide.region_6.10_spmd.clone.sunk | while | flops 43772256 | bytes 16048483 | solution.py:169
  331.0 0.8 compare_and_fusion.11
  331.7 4.0 gather_fusion.1
  335.7 4.0 gather_fusion
  342.9 0.8 compare_and_fusion.11
  343.6 4.0 gather_fusion.1
  347.6 4.0 gather_fusion
  354.1 69.7 %pmax.7 = f32[4,8,20]{2,1,0:T(8,128)S(1)} all-reduce(f32[4,8,20]{2,1,0:T(8,128)S(1)} %pad_maximum_fusion), channel_id=1, replica_groups=mesh['grp'=8,'seq'=16] {'seq'}, use_global_device_ids=true, to_apply=%region_28.30 | all-reduce | flops 640 | bytes 5120 | tf_op jit(solution)/shard_map/pmax | solution.py:176
  423.9 1.7 fusion.71
  425.7 36.1 %psum.44 = bf16[4,8,20]{2,1,0:T(8,128)(2,1)S(1)} all-reduce(bf16[4,8,20]{2,1,0:T(8,128)(2,1)S(1)} %get-tuple-element.666), channel_id=1, replica_groups=mesh['grp'=8,'seq'=16] {'seq'}, use_global_device_ids=true, to_apply=%region_30.32 | all-reduce | flops 640 | bytes 2560 | tf_op jit(solution)/shard_map/psum | solution.py:179
  461.9 70.2 %all-reduce.10.cloned.1.call-done = bf16[4,8,20,128]{3,1,2,0:T(8,128)(2,1)} async-done(((bf16[4,8,20,128]{3,1,2,0:T(8,128)(2,1)}), bf16[4,8,20,128]{3,1,2,0:T(8,128)(2,1)}) %all-reduce.10.cloned.1.call-update) | async-done | bytes 163856 | tf_op jit(solution)/shard_map/psum | solution.py:180
  532.0 1.1 divide_convert_fusion
  533.4 13.0 %all_gather.14 = bf16[32,4,320]{2,1,0:T(4,128)(2,1)S(1)} all-gather(bf16[4,4,320]{2,1,0:T(4,128)(2,1)S(1)} %constant_dynamic-slice_fusion), channel_id=1, replica_groups=mesh['grp'=8,'seq'=16] {'grp'}, dimensions={0}, use_global_device_ids=true | all-gather | bytes 92160 | tf_op jit(solution)/shard_map/all_gather | solution.py:192
  546.4 1.9 convolution_convert_fusion.2
  548.4 1.2 dynamic-slice.2
  549.6 1.7 sort.17
  552.0 78.8 %all-reduce.14.cloned.1.call-done = bf16[32,4,640]{2,0,1:T(8,128)(2,1)} async-done(((bf16[32,4,640]{2,0,1:T(8,128)(2,1)}), bf16[32,4,640]{2,0,1:T(8,128)(2,1)}) %all-reduce.14.cloned.1.call-update) | async-done | bytes 163856
  630.8 1.0 multiply_reduce_fusion
  631.8 62.7 %psum.45 = f32[32,4]{0,1:T(4,128)S(1)} all-reduce(f32[32,4]{0,1:T(4,128)S(1)} %multiply_reduce_fusion), channel_id=1, replica_groups=mesh['grp'=8,'seq'=16] {'grp','seq'}, use_global_device_ids=true, to_apply=%region_33.35 | all-reduce | flops 128 | bytes 1024 | tf_op jit(solution)/shard_map/psum | solution.py:200
  694.5 0.9 multiply_convert_fusion
  695.6 23.7 %all_gather.15 = bf16[32,4,640]{0,1,2:T(4,128)(2,1)S(1)} all-gather(bf16[32,4,40]{0,1,2:T(4,128)(2,1)S(1)} %copy.213), channel_id=1, replica_groups=mesh['grp'=8,'seq'=16] {'seq'}, dimensions={2}, use_global_device_ids=true | all-gather | bytes 174080 | tf_op jit(solution)/shard_map/all_gather | solution.py:204
  719.7 1.2 convolution_convert_fusion
  720.8 1.1 convolution_convert_fusion.1
  722.1 58.0 %all-reduce.18.cloned.1.call-done = (bf16[32,4,864]{2,0,1:T(8,128)(2,1)}, bf16[32,4,864]{2,0,1:T(8,128)(2,1)}) async-done(((bf16[32,4,864]{2,0,1:T(8,128)(2,1)}, bf16[32,4,864]{2,0,1:T(8,128)(2,1)}), (bf16[32,4,864]{2,0,1:T(8,128)(2,1)}, bf16[32,4,864]{2,0,1:T(8,128)(2,1)})) %all-reduce.18.cloned.1.call-update) | async-done | bytes 442384 | tf_op jit(solution)/shard_map/psum | solution.py:209
  780.0 2.5 convolution_convert_fusion.3
  782.6 84.0 %all-reduce.16.cloned.1.call-done = bf16[32,4,640]{2,0,1:T(8,128)(2,1)} async-done(((bf16[32,4,640]{2,0,1:T(8,128)(2,1)}), bf16[32,4,640]{2,0,1:T(8,128)(2,1)}) %all-reduce.16.cloned.1.call-update) | async-done | bytes 163856
  866.6 1.0 convert_add_fusion.1
  (172 shorter events, 29.8 us)
Async XLA Ops:
  6.5 713.1 %copy-start = (bf16[640,864]{0,1:T(8,128)(2,1)S(1)}, bf16[640,864]{0,1:T(8,128)(2,1)}, u32[]{:S(2)}) copy-start(bf16[640,864]{0,1:T(8,128)(2,1)} %param.36) | copy-start | bytes 3317764
  6.5 154.0 %all-reduce.12.cloned.1.call-start = ((), (), s32[]{:S(2)}) async-start(), calls=%async_computation.1 | async-start | bytes 262144
  7.3 70.4 %copy-start.8 = (pred[32]{0:T(512)(128)(4,1)}, pred[32]{0:T(512)(128)(4,1)S(1)}, u32[]{:S(2)}) copy-start(pred[32]{0:T(512)(128)(4,1)S(1)} %compare_and_fusion.5) | copy-start | bytes 100
  102.5 429.5 %all-reduce.10.cloned.1.call-start = ((), (), s32[]{:S(2)}) async-start(), calls=%async_computation | async-start | bytes 327680 | tf_op jit(solution)/shard_map/psum | solution.py:180
  106.8 208.1 %copy-start.5 = (pred[20,4]{0,1:T(4,128)(4,1)}, pred[20,4]{0,1:T(4,128)(4,1)S(1)}, u32[]{:S(2)}) copy-start(pred[20,4]{0,1:T(4,128)(4,1)S(1)} %fusion.119) | copy-start | bytes 244
  270.4 9.5 %copy-start.2 = (f32[8,20,4]{1,2,0:T(4,128)}, f32[8,20,4]{1,2,0:T(4,128)S(1)}, u32[]{:S(2)}) copy-start(f32[8,20,4]{1,2,0:T(4,128)S(1)} %get-tuple-element.733) | copy-start | bytes 7684
  270.8 7.8 copy-start.6
  271.1 7.5 copy-start.7
  325.8 1.2 copy-start.4
  330.2 219.4 %copy-start.11 = (s32[32]{0:T(128)S(1)}, s32[32]{0:T(128)}, u32[]{:S(2)}) copy-start(s32[32]{0:T(128)} %param.26) | copy-start | bytes 388
  330.3 300.5 %copy-start.9 = (pred[32]{0:T(512)(128)(4,1)S(1)}, pred[32]{0:T(512)(128)(4,1)}, u32[]{:S(2)}) copy-start(pred[32]{0:T(512)(128)(4,1)} %copy-done.8) | copy-start | bytes 100
  330.3 364.3 %copy-start.10 = (f32[40]{0:T(128)S(1)}, f32[40]{0:T(128)}, u32[]{:S(2)}) copy-start(f32[40]{0:T(128)} %param.34) | copy-start | bytes 484
  339.7 0.8 copy-start.3
  351.6 0.8 copy-start.3
  354.1 366.7 %copy-start.1 = (bf16[640,864]{0,1:T(8,128)(2,1)S(1)}, bf16[640,864]{0,1:T(8,128)(2,1)}, u32[]{:S(2)}) copy-start(bf16[640,864]{0,1:T(8,128)(2,1)} %param.35) | copy-start | bytes 3317764
  425.6 205.1 %all-reduce.14.cloned.1.call-start = ((), (), s32[]{:S(2)}) async-start(), calls=%async_computation.2 | async-start | bytes 327680
  548.3 231.7 %all-reduce.18.cloned.1.call-start = ((), (), s32[]{:S(2)}) async-start(), calls=%async_computation.4 | async-start | bytes 917504 | tf_op jit(solution)/shard_map/psum | solution.py:209
  722.0 144.6 %all-reduce.16.cloned.1.call-start = ((), (), s32[]{:S(2)}) async-start(), calls=%async_computation.3 | async-start | bytes 327680
Sparse Core Ops, SparseCore 0:
  102.6 57.7 all-reduce.11
  425.8 106.2 all-reduce.9
  548.5 82.2 all-reduce.13
  722.1 57.8 all-reduce.17
  783.1 83.4 all-reduce.15
where the time goes:
time: 878 us; the launch traced here: 875 us
  blocking collectives  375 us (43%)
  waiting for transfers between devices  339 us (39%)
  local copies, waits for them, and re-layouts  93.7 us (11%)
  other arithmetic  29.9 us (3%)
  matrix products  18.9 us (2%)
  between operations  17.5 us (2%)
    unnamed x8, waiting for transfers between devices  211 us
    all_gather x1, blocking collectives, body(): proj_full = lax.all_gather(proj_share, 'seq', axis=2, tiled=True)  80 us
    psum x1, waiting for transfers between devices, body(): lax.psum((weighted * factor[..., None]).astype(jnp.bfloat16), 'seq')  70.2 us
    pmax x1, blocking collectives, body(): top_score = lax.pmax(best_score, 'seq')  69.7 us
    psum x1, blocking collectives, body(): lax.psum(jnp.sum(sorted_rows * sorted_rows, axis=-1), ('grp', 'seq'))  68.2 us
    psum x1, blocking collectives, body(): lax.psum(jnp.sum(residual * residual, axis=-1), ('grp', 'seq'))  62.7 us
    psum x1, waiting for transfers between devices, body(): lax.psum(up_part.astype(jnp.bfloat16), 'grp').astype(jnp.float32)  58 us
    psum x1, blocking collectives, body(): lax.psum((weight_sums * factor).astype(jnp.bfloat16), 'seq')  36.1 us
  transfers between devices with their start and end apart: 5, of which 5 were waited for; matrix products, arithmetic and copies ran while one was open for 1% of the time, Pallas kernels for 0%

commit v1 on v0

--- a/solution.py
+++ b/solution.py
@@ -15,6 +15,19 @@
 EPSILON = 1e-06
 LOW_SCORE = -1e30
 ROPE_BASE = 1000000.0
+
+
+def show_patches(t0, device_axis):
+    r1 = jnp.concatenate(
+        lax.all_to_all(
+            jnp.stack([t0] * lax.axis_size(device_axis)),
+            axis_name=device_axis,
+            split_axis=0,
+            concat_axis=0,
+        ),
+        axis=2,
+    )
+    return r1
 
 
 def rotary(values, position):
@@ -96,7 +109,7 @@
         ).astype(jnp.float32)
         + qkv_bias
     )
-    proj_full = lax.all_gather(proj_share, "seq", axis=2, tiled=True)
+    proj_full = show_patches(proj_share, "seq")
     members = lax.dynamic_slice_in_dim(group_perm, grp_idx * REQ_GRP, REQ_GRP)
     my_lengths = jnp.take(lengths, members)
     steps_range = jnp.arange(STEPS, dtype=jnp.int32)

time: 878 us -> 787 us (0.90)
  blocking collectives: 375 us -> 295 us
  local copies, waits for them, and re-layouts: 93.7 us -> 63.8 us
  waiting for transfers between devices: 339 us -> 352 us
    all_gather x1 -> x0, blocking collectives: 80 us -> none  [body(): proj_full = lax.all_gather(proj_share, 'seq', axis=2, tiled=True)]
    slice x9 -> x0, local copies, waits for them, and re-layouts: 21 us -> none  [the longest x2 9.53 us: rotary(): second_half = values[..., half_dim:]]
    unnamed x26 -> x38, local copies, waits for them, and re-layouts: 11.6 us -> 1.26 us
    all_to_all x0 -> x1, waiting for transfers between devices: none -> 9.88 us  [show_patches(): lax.all_to_all(jnp.stack([t0] * lax.axis_size(device_axis)), axis_name=de...]
  transfers between devices with their start and end apart: 5 -> 6, of which waited for: 5 -> 6; matrix products, arithmetic and copies ran while one was open for 1% -> 1% of each run, Pallas kernels for 0% -> 0%
where the time goes in v1:
time: 787 us; the launch traced here: 785 us
  waiting for transfers between devices  352 us (45%)
  blocking collectives  295 us (37%)
  local copies, waits for them, and re-layouts  63.8 us (8%)
  other arithmetic  29.3 us (4%)
  matrix products  18.6 us (2%)
  between operations  17.6 us (2%)
    unnamed x8, waiting for transfers between devices  215 us
    psum x1, waiting for transfers between devices, body(): lax.psum((weighted * factor[..., None]).astype(jnp.bfloat16), 'seq')  69.7 us
    pmax x1, blocking collectives, body(): top_score = lax.pmax(best_score, 'seq')  69.5 us
    psum x1, blocking collectives, body(): lax.psum(jnp.sum(sorted_rows * sorted_rows, axis=-1), ('grp', 'seq'))  68.2 us
    psum x1, blocking collectives, body(): lax.psum(jnp.sum(residual * residual, axis=-1), ('grp', 'seq'))  62.7 us
    psum x1, waiting for transfers between devices, body(): lax.psum(up_part.astype(jnp.bfloat16), 'grp').astype(jnp.float32)  58 us
    psum x1, blocking collectives, body(): lax.psum((weight_sums * factor).astype(jnp.bfloat16), 'seq')  36.1 us
    gather x6, local copies, waits for them, and re-layouts, advance(): jnp.take(v_pool, slot_ids, axis=0).reshape(block_rows, KV_HEADS, HEAD_DIM)  24 us
  transfers between devices with their start and end apart: 6, of which 6 were waited for; matrix products, arithmetic and copies ran while one was open for 1% of the time, Pallas kernels for 0%

profile of v1, /device:TPU:0, one launch (start us, length us, event | category | flops | bytes accessed | tf_op | source)
XLA Modules:
  0.0 784.7 jit_solution(15766375314973922299)
XLA Ops:
  6.5 0.7 compare_select_fusion.5
  8.0 1.4 gather_fusion.8
  9.5 68.2 %psum.42 = f32[32,4]{0,1:T(4,128)S(1)} all-reduce(f32[32,4]{0,1:T(4,128)S(1)} %fusion.75), channel_id=1, replica_groups=mesh['grp'=8,'seq'=16] {'grp','seq'}, use_global_device_ids=true, to_apply=%region_2.3 | all-reduce | flops 128 | bytes 1024 | tf_op jit(solution)/shard_map/psum | solution.py:96
  77.7 0.7 fusion.77
  78.6 21.7 %all_gather.9 = bf16[32,4,640]{0,1,2:T(4,128)(2,1)S(1)} all-gather(bf16[32,4,40]{0,1,2:T(4,128)(2,1)S(1)} %copy.107), channel_id=1, replica_groups=mesh['grp'=8,'seq'=16] {'seq'}, dimensions={2}, use_global_device_ids=true | all-gather | bytes 174080 | tf_op jit(solution)/shard_map/all_gather | solution.py:102
  100.3 2.2 convolution_convert_fusion.4
  109.3 51.3 %all-reduce.12.cloned.1.call-done = bf16[32,4,448]{2,0,1:T(8,128)(2,1)} async-done(((bf16[32,4,448]{2,0,1:T(8,128)(2,1)}), bf16[32,4,448]{2,0,1:T(8,128)(2,1)}) %all-reduce.12.cloned.1.call-update) | async-done | bytes 114704
  160.6 0.8 convert_add_fusion.2
  161.4 0.9 stack.64
  162.3 7.0 all-to-all-start
  169.5 9.9 %all-to-all-done = f32[16,4,4,448]{3,2,1,0:T(4,128)S(1)} async-done(((f32[16,4,4,448]{3,2,1,0:T(4,128)}), f32[16,4,4,448]{3,2,1,0:T(4,128)S(1)}, u32[]{:S(2)}, u32[]{:S(2)}) %all-to-all-start) | async-done | bytes 458784 | tf_op jit(solution)/shard_map/all_to_all | solution.py:22
  184.6 24.4 %while.63 = (s32[]{:T(128)}, f32[8,20]{1,0:T(8,128)S(1)}, f32[8,20]{1,0:T(8,128)S(1)}, f32[8,20,128]{2,1,0:T(8,128)S(1)}, s32[]{:T(128)}, /*index=5*/s32[]{:T(12...) while((s32[]{:T(128)}, f32[8,20]{1,0:T(8,128)S(1)}, ...), condition=%wide.region_27.29_spmd.clone, body=%wide.region_24.28_spmd.clone.sunk | while | flops 43772256 | bytes 20078948 | solution.py:182
  184.7 4.0 gather_fusion.6
  188.8 4.0 gather_fusion.7
  192.8 1.2 broadcast_select_fusion.18
  194.9 0.7 fusion.196
  196.9 4.0 gather_fusion.6
  200.9 4.0 gather_fusion.7
  204.9 1.2 broadcast_select_fusion.18
  207.1 0.7 fusion.196
  209.0 0.9 convolution_add_fusion.5
  209.9 12.4 %while.62 = (s32[]{:T(128)}, f32[8,20]{1,0:T(8,128)S(1)}, f32[8,20]{1,0:T(8,128)S(1)}, f32[8,20,128]{2,1,0:T(8,128)S(1)}, s32[]{:T(128)}, /*index=5*/s32[]{:T(12...) while((s32[]{:T(128)}, f32[8,20]{1,0:T(8,128)S(1)}, ...), condition=%wide.region_21.23_spmd.clone, body=%wide.region_18.22_spmd.clone.sunk | while | flops 43772256 | bytes 20243128 | solution.py:182
  210.1 4.0 gather_fusion.4
  214.1 4.0 gather_fusion.5
  218.1 1.2 broadcast_select_fusion.17
  220.3 0.7 fusion.190
  222.4 1.3 exponential_multiply_fusion.2
  223.7 0.9 convolution_add_fusion.6
  224.6 12.8 %while.61 = (s32[]{:T(128)}, f32[8,20]{1,0:T(8,128)S(1)}, f32[8,20]{1,0:T(8,128)S(1)}, f32[8,20,128]{2,1,0:T(8,128)S(1)}, s32[]{:T(128)}, /*index=5*/s32[]{:T(12...) while((s32[]{:T(128)}, f32[8,20]{1,0:T(8,128)S(1)}, ...), condition=%wide.region_15.17_spmd.clone, body=%wide.region_12.16_spmd.clone.sunk | while | flops 43772256 | bytes 20242816 | solution.py:182
  224.7 0.7 compare_and_fusion.12
  225.4 4.0 gather_fusion.2
  229.4 4.0 gather_fusion.3
  233.4 1.2 broadcast_select_fusion.16
  235.6 0.7 fusion.184
  238.1 0.9 convolution_add_fusion.7
  239.0 25.8 %while.60 = (s32[]{:T(128)}, f32[8,20]{1,0:T(8,128)S(1)}, f32[8,20]{1,0:T(8,128)S(1)}, f32[8,20,128]{2,1,0:T(8,128)S(1)}, s32[]{:T(128)}, /*index=5*/s32[]{:T(12...) while((s32[]{:T(128)}, f32[8,20]{1,0:T(8,128)S(1)}, ...), condition=%wide.region_9.11_spmd.clone, body=%wide.region_6.10_spmd.clone.sunk | while | flops 43772256 | bytes 20242816 | solution.py:182
  239.9 4.0 gather_fusion
  243.9 4.0 gather_fusion.1
  247.9 1.2 broadcast_select_fusion.15
  250.1 0.7 fusion.178
  252.7 4.0 gather_fusion
  256.7 4.0 gather_fusion.1
  260.7 1.2 broadcast_select_fusion.15
  262.9 0.7 fusion.178
  264.9 69.5 %pmax.7 = f32[4,8,20]{2,1,0:T(8,128)S(1)} all-reduce(f32[4,8,20]{2,1,0:T(8,128)S(1)} %pad_maximum_fusion), channel_id=1, replica_groups=mesh['grp'=8,'seq'=16] {'seq'}, use_global_device_ids=true, to_apply=%region_28.30 | all-reduce | flops 640 | bytes 5120 | tf_op jit(solution)/shard_map/pmax | solution.py:189
  334.5 1.7 fusion.71
  336.3 36.1 %psum.44 = bf16[4,8,20]{2,1,0:T(8,128)(2,1)S(1)} all-reduce(bf16[4,8,20]{2,1,0:T(8,128)(2,1)S(1)} %get-tuple-element.622), channel_id=1, replica_groups=mesh['grp'=8,'seq'=16] {'seq'}, use_global_device_ids=true, to_apply=%region_30.32 | all-reduce | flops 640 | bytes 2560 | tf_op jit(solution)/shard_map/psum | solution.py:192
  372.6 69.7 %all-reduce.10.cloned.1.call-done = bf16[4,8,20,128]{3,1,2,0:T(8,128)(2,1)} async-done(((bf16[4,8,20,128]{3,1,2,0:T(8,128)(2,1)}), bf16[4,8,20,128]{3,1,2,0:T(8,128)(2,1)}) %all-reduce.10.cloned.1.call-update) | async-done | bytes 163856 | tf_op jit(solution)/shard_map/psum | solution.py:193
  442.3 1.1 divide_convert_fusion
  443.6 13.0 %all_gather.10 = bf16[32,4,320]{2,1,0:T(4,128)(2,1)S(1)} all-gather(bf16[4,4,320]{2,1,0:T(4,128)(2,1)S(1)} %constant_dynamic-slice_fusion), channel_id=1, replica_groups=mesh['grp'=8,'seq'=16] {'grp'}, dimensions={0}, use_global_device_ids=true | all-gather | bytes 92160 | tf_op jit(solution)/shard_map/all_gather | solution.py:205
  456.6 0.9 convolution_convert_fusion.2
  458.2 1.6 sort.17
  460.5 79.5 %all-reduce.14.cloned.1.call-done = bf16[32,4,640]{2,0,1:T(8,128)(2,1)} async-done(((bf16[32,4,640]{2,0,1:T(8,128)(2,1)}), bf16[32,4,640]{2,0,1:T(8,128)(2,1)}) %all-reduce.14.cloned.1.call-update) | async-done | bytes 163856
  540.0 1.0 multiply_reduce_fusion
  541.0 62.7 %psum.45 = f32[32,4]{0,1:T(4,128)S(1)} all-reduce(f32[32,4]{0,1:T(4,128)S(1)} %multiply_reduce_fusion), channel_id=1, replica_groups=mesh['grp'=8,'seq'=16] {'grp','seq'}, use_global_device_ids=true, to_apply=%region_33.35 | all-reduce | flops 128 | bytes 1024 | tf_op jit(solution)/shard_map/psum | solution.py:213
  603.8 0.9 multiply_convert_fusion
  604.8 23.7 %all_gather.11 = bf16[32,4,640]{0,1,2:T(4,128)(2,1)S(1)} all-gather(bf16[32,4,40]{0,1,2:T(4,128)(2,1)S(1)} %copy.133), channel_id=1, replica_groups=mesh['grp'=8,'seq'=16] {'seq'}, dimensions={2}, use_global_device_ids=true | all-gather | bytes 174080 | tf_op jit(solution)/shard_map/all_gather | solution.py:217
  628.9 1.2 convolution_convert_fusion
  630.1 1.1 convolution_convert_fusion.1
  631.3 58.0 %all-reduce.18.cloned.1.call-done = (bf16[32,4,864]{2,0,1:T(8,128)(2,1)}, bf16[32,4,864]{2,0,1:T(8,128)(2,1)}) async-done(((bf16[32,4,864]{2,0,1:T(8,128)(2,1)}, bf16[32,4,864]{2,0,1:T(8,128)(2,1)}), (bf16[32,4,864]{2,0,1:T(8,128)(2,1)}, bf16[32,4,864]{2,0,1:T(8,128)(2,1)})) %all-reduce.18.cloned.1.call-update) | async-done | bytes 442384 | tf_op jit(solution)/shard_map/psum | solution.py:222
  689.3 2.5 convolution_convert_fusion.3
  691.9 84.0 %all-reduce.16.cloned.1.call-done = bf16[32,4,640]{2,0,1:T(8,128)(2,1)} async-done(((bf16[32,4,640]{2,0,1:T(8,128)(2,1)}), bf16[32,4,640]{2,0,1:T(8,128)(2,1)}) %all-reduce.16.cloned.1.call-update) | async-done | bytes 163856
  775.8 1.0 convert_add_fusion.1
  777.4 0.7 select_convert_fusion
  (199 shorter events, 26.7 us)
Async XLA Ops:
  6.5 622.4 %copy-start = (bf16[640,864]{0,1:T(8,128)(2,1)S(1)}, bf16[640,864]{0,1:T(8,128)(2,1)}, u32[]{:S(2)}) copy-start(bf16[640,864]{0,1:T(8,128)(2,1)} %param.36) | copy-start | bytes 3317764
  6.5 154.0 %all-reduce.12.cloned.1.call-start = ((), (), s32[]{:S(2)}) async-start(), calls=%async_computation.2 | async-start | bytes 262144
  8.0 70.5 %copy-start.19 = (pred[32]{0:T(512)(128)(4,1)}, pred[32]{0:T(512)(128)(4,1)S(1)}, u32[]{:S(2)}) copy-start(pred[32]{0:T(512)(128)(4,1)S(1)} %compare_and_fusion.5) | copy-start | bytes 100
  78.6 24.0 %copy-start.23 = (s32[32]{0:T(128)S(1)}, s32[32]{0:T(128)}, u32[]{:S(2)}) copy-start(s32[32]{0:T(128)} %param.26) | copy-start | bytes 388
  78.6 24.1 %copy-start.1 = (s32[32]{0:T(128)S(1)}, s32[32]{0:T(128)}, u32[]{:S(2)}) copy-start(s32[32]{0:T(128)} %param.25) | copy-start | bytes 388
  100.3 6.4 copy-start.16
  100.3 7.7 copy-start.26
  100.3 60.2 %copy-start.21 = (f32[448]{0:T(512)S(1)}, f32[448]{0:T(512)}, u32[]{:S(2)}) copy-start(f32[448]{0:T(512)} %param.32) | copy-start | bytes 5380
  162.3 17.1 %all-to-all-start = ((f32[16,4,4,448]{3,2,1,0:T(4,128)}), f32[16,4,4,448]{3,2,1,0:T(4,128)S(1)}, u32[]{:S(2)}, u32[]{:S(2)}) async-start(f32[16,4,4,448]{3,2,1,0:T(4,128)} %stack.64), calls=%async_computation | async-start | bytes 1048576 | tf_op jit(solution)/shard_map/all_to_all | solution.py:22
  169.2 273.0 %all-reduce.10.cloned.1.call-start = ((), (), s32[]{:S(2)}) async-start(), calls=%async_computation.1 | async-start | bytes 327680 | tf_op jit(solution)/shard_map/psum | solution.py:193
  169.3 54.4 %copy-start.13 = (pred[20,4]{0,1:T(4,128)(4,1)}, pred[20,4]{0,1:T(4,128)(4,1)S(1)}, u32[]{:S(2)}) copy-start(pred[20,4]{0,1:T(4,128)(4,1)S(1)} %fusion.115) | copy-start | bytes 244
  180.1 4.3 copy-start.8
  182.2 1.5 copy-start.17
  182.2 2.4 copy-start.9
  183.1 0.6 copy-start.18
  194.9 1.2 copy-start.2
  207.1 1.2 copy-start.2
  210.0 4.1 copy-start.14
  219.3 0.9 copy-start.12
  220.2 1.2 copy-start.3
  221.7 0.6 copy-start.15
  234.6 0.9 copy-start.11
  235.6 1.2 copy-start.4
  249.2 0.9 copy-start.10
  250.1 1.2 copy-start.5
  262.0 0.9 copy-start.10
  262.9 1.2 copy-start.5
  334.4 122.2 %copy-start.7 = (bf16[320,640]{1,0:T(8,128)(2,1)S(1)}, bf16[320,640]{1,0:T(8,128)(2,1)}, u32[]{:S(2)}) copy-start(bf16[320,640]{1,0:T(8,128)(2,1)} %param.33) | copy-start | bytes 1228804
  336.3 203.8 %all-reduce.14.cloned.1.call-start = ((), (), s32[]{:S(2)}) async-start(), calls=%async_computation.3 | async-start | bytes 327680
  372.5 85.1 %copy-start.25 = (u32[128]{0:T(128)S(1)}, u32[128]{0:T(128)}, u32[]{:S(2)}) copy-start(u32[128]{0:T(128)} %constant.254) | copy-start | bytes 1540
  372.5 85.7 %copy-start.24 = (s32[32]{0:T(128)S(1)}, s32[32]{0:T(128)}, u32[]{:S(2)}) copy-start(s32[32]{0:T(128)} %param.26) | copy-start | bytes 388
  372.5 167.5 %copy-start.20 = (pred[32]{0:T(512)(128)(4,1)S(1)}, pred[32]{0:T(512)(128)(4,1)}, u32[]{:S(2)}) copy-start(pred[32]{0:T(512)(128)(4,1)} %copy-done.19) | copy-start | bytes 100
  372.5 231.2 %copy-start.22 = (f32[40]{0:T(128)S(1)}, f32[40]{0:T(128)}, u32[]{:S(2)}) copy-start(f32[40]{0:T(128)} %param.34) | copy-start | bytes 484
  457.6 231.7 %all-reduce.18.cloned.1.call-start = ((), (), s32[]{:S(2)}) async-start(), calls=%async_computation.5 | async-start | bytes 917504 | tf_op jit(solution)/shard_map/psum | solution.py:222
  628.5 1.5 copy-start.6
  631.2 144.6 %all-reduce.16.cloned.1.call-start = ((), (), s32[]{:S(2)}) async-start(), calls=%async_computation.4 | async-start | bytes 327680
Sparse Core Ops, SparseCore 0:
  102.7 57.7 all-reduce.11
  336.4 105.8 all-reduce.9
  457.7 82.3 all-reduce.13
  631.3 57.8 all-reduce.17
  692.4 83.4 all-reduce.15
